TPU v7x, 256 devices: a whole 4x4x8 slice. The times are simulated.
256 devices in a mesh: seq: 32 (over y, z), head: 8 (over x, core).
Axes of the slice: x: 4, y: 4, z: 8, core: 2. Of those that a mesh axis runs over, the one named last changes fastest.
Arguments:
- inputs: bfloat16 [8192, 8192], P('seq'), may hold values from -6 to 6
- w_value: bfloat16 [8192, 4096], P('seq', 'head'), may hold values from -0.0625 to 0.0625
- log_decay: float32 [8192, 64], P('seq', 'head'), may hold values from -1 to 0
- b_proj: bfloat16 [8192, 128], P('seq'), may hold values from -0.5 to 0.5
- c_proj: bfloat16 [8192, 128], P('seq'), may hold values from -0.5 to 0.5
- grad_out: bfloat16 [8192, 4096], P('seq', 'head'), may hold values from -6 to 6
Outputs:
- grad_input: bfloat16 [8192, 8192], P('seq', 'head')
- grad_weight: float32 [8192, 4096], P('seq', 'head')
- grad_b: float32 [8192, 128], P('seq')
- grad_c: float32 [8192, 128], P('seq')
All inputs are finite; a program needn't handle non-finite values.
Results may differ from a plain program's by a relative error of at most 0.027.
Values may be sent and summed in bfloat16 or wider, within the bound.
A program may use at most 128 MiB of HBM per device.

v0:
```python
import jax
import jax.numpy as jnp
from jax import lax
from jax.sharding import PartitionSpec as P

SPAN = 256
HIGH = lax.Precision.HIGHEST


def carried_in(array, axis, combine, identity, reverse):
    length, index = (lax.axis_size(axis), lax.axis_index(axis))
    everything = jax.tree.map(
        lambda part, kind: lax.all_gather(part.astype(kind), axis),
        array,
        (jnp.bfloat16, jnp.bfloat16),
    )
    start = jax.tree.map(
        lambda part, zero: jnp.broadcast_to(jnp.asarray(zero, part.dtype), part.shape),
        array,
        identity,
    )

    def lap(k, before):
        at = length - 1 - k if reverse else k
        reached = at > index if reverse else at < index
        new = combine(
            before, jax.tree.map(lambda part, own: part[at].astype(own.dtype), everything, array)
        )
        return jax.tree.map(lambda a, b: jnp.where(reached, a, b), new, before)

    return lax.fori_loop(0, length, lap, start)


def link(earlier, later):
    return (earlier[0] * later[0], later[0][:, None, None] * earlier[1] + later[1])


def advance_once(carried, item):
    decay, local = item
    return (decay[:, None, None] * carried + local, carried)


def per_device(inputs, w_value, log_decay, b_proj, c_proj, grad_out):
    steps = inputs.shape[0]
    heads = log_decay.shape[1]
    columns = grad_out.shape[1]
    depth = columns // heads
    states = b_proj.shape[1]
    blocks = steps // SPAN
    w_full = lax.all_gather(w_value, "seq", axis=0, tiled=True)
    values = jnp.dot(inputs, w_full, preferred_element_type=jnp.float32).astype(jnp.bfloat16)
    xs = values.astype(jnp.float32).reshape(blocks, SPAN, heads, depth)
    dys = grad_out.astype(jnp.float32).reshape(blocks, SPAN, heads, depth)
    bs = b_proj.astype(jnp.float32).reshape(blocks, SPAN, states)
    cs = c_proj.astype(jnp.float32).reshape(blocks, SPAN, states)
    before_or_at = jnp.tril(jnp.ones((SPAN, SPAN), jnp.float32))
    cum_log = jnp.einsum(
        "tj,kjh->kth", before_or_at, log_decay.reshape(blocks, SPAN, heads), precision=HIGH
    )
    totals = cum_log[:, -1]
    grow = jnp.exp(cum_log)
    shrink = jnp.exp(totals[:, None] - cum_log)
    cum_heads = jnp.swapaxes(cum_log, 1, 2)
    rows = lax.broadcasted_iota(jnp.int32, (SPAN, SPAN), 0)
    cols = lax.broadcasted_iota(jnp.int32, (SPAN, SPAN), 1)
    lower = (rows >= cols)[None, None]
    diff = cum_heads[:, :, :, None] - cum_heads[:, :, None, :]
    decay_mat = jnp.exp(jnp.where(lower, diff, -jnp.inf))
    cross = jnp.einsum("kthp,kjhp->khtj", dys, xs, precision=HIGH)
    mixed = decay_mat * cross
    scores = jnp.einsum("ktn,kjn->ktj", cs, bs, precision=HIGH)
    span_decay = jnp.exp(totals)
    dev_decay = jnp.exp(jnp.sum(totals, axis=0))
    zero_state = jnp.zeros((heads, depth, states), jnp.float32)
    identity_matrix = (jnp.ones_like(dev_decay), zero_state)
    local_end = jnp.einsum("kjhp,kjh,kjn->khpn", xs, shrink, bs, precision=HIGH)
    dev_state, before = lax.scan(advance_once, zero_state, (span_decay, local_end))
    incoming = carried_in((dev_decay, dev_state), "seq", link, identity_matrix, False)[1]
    earlier = jnp.tril(jnp.ones((blocks, blocks), jnp.float32))
    through = jnp.einsum("kl,lh->kh", earlier, totals, precision=HIGH)
    lead = jnp.exp(through - totals)
    state_in = before + lead[:, :, None, None] * incoming[None]
    grad_c = jnp.einsum("kthp,khpn,kth->ktn", dys, state_in, grow, precision=HIGH)
    grad_c = grad_c + jnp.einsum("khtj,kjn->ktn", mixed, bs, precision=HIGH)
    local_back = jnp.einsum("kthp,kth,ktn->khpn", dys, grow, cs, precision=HIGH)
    dev_back, after = lax.scan(advance_once, zero_state, (span_decay, local_back), reverse=True)
    incoming_back = carried_in((dev_decay, dev_back), "seq", link, identity_matrix, True)[1]
    trail = jnp.exp(jnp.sum(totals, axis=0)[None] - through)
    grad_in = after + trail[:, :, None, None] * incoming_back[None]
    grad_vals = jnp.einsum("khst,kst,kshp->kthp", decay_mat, scores, dys, precision=HIGH)
    grad_vals = grad_vals + jnp.einsum("khpn,ktn,kth->kthp", grad_in, bs, shrink, precision=HIGH)
    grad_b = jnp.einsum("khst,ksn->ktn", mixed, cs, precision=HIGH)
    grad_b = grad_b + jnp.einsum("kthp,khpn,kth->ktn", xs, grad_in, shrink, precision=HIGH)
    grad_values = grad_vals.reshape(steps, columns).astype(jnp.bfloat16)
    grad_b, grad_c = (
        lax.psum(grad_b.reshape(steps, states).astype(jnp.bfloat16), "head").astype(jnp.float32),
        lax.psum(grad_c.reshape(steps, states).astype(jnp.bfloat16), "head").astype(jnp.float32),
    )
    term = lax.dot_general(
        grad_values, w_full, (((1,), (1,)), ((), ())), preferred_element_type=jnp.float32
    )
    grad_input = lax.psum_scatter(
        term.astype(jnp.bfloat16), "head", scatter_dimension=1, tiled=True
    )
    grad_weight = lax.psum_scatter(
        lax.dot_general(
            inputs, grad_values, (((0,), (0,)), ((), ())), preferred_element_type=jnp.float32
        ).astype(jnp.bfloat16),
        "seq",
        scatter_dimension=0,
        tiled=True,
    ).astype(jnp.float32)
    return (grad_input, grad_weight, grad_b, grad_c)


def solution(mesh):
    placed = (
        P("seq", None),
        P("seq", "head"),
        P("seq", "head"),
        P("seq", None),
        P("seq", None),
        P("seq", "head"),
    )
    return jax.shard_map(
        per_device,
        mesh=mesh,
        in_specs=placed,
        out_specs=(P("seq", "head"), P("seq", "head"), P("seq", None), P("seq", None)),
        check_vma=False,
    )
```

profile of v0, /device:TPU:8, one launch (start us, length us, event | category | flops | bytes accessed | tf_op | source)
XLA Modules:
  0.0 656.2 jit_solution(16976083974051187872)
XLA Ops:
  8.0 1.1 copy.24
  10.2 1.9 fusion.18
  12.4 41.5 %all-gather = bf16[32,1,8]{2,1,0:T(2,128)(2,1)S(1)} all-gather(bf16[1,1,8]{2,1,0:T(2,128)(2,1)S(1)} %copy.26), channel_id=2, replica_groups=mesh['seq'=32,'head'=8] {'seq'}, dimensions={0}, use_global_device_ids=true | all-gather | bytes 528 | tf_op jit(solution)/shard_map/all_gather | solution.py:13
  53.9 1.0 fusion.47
  55.0 55.8 %all-gather.7.cloned.1.call-done = bf16[8192,512]{1,0:T(8,128)(2,1)} async-done(((bf16[256,512]{1,0:T(8,128)(2,1)}), bf16[8192,512]{1,0:T(8,128)(2,1)}) %all-gather.7.cloned.1.call-update) | async-done | bytes 8388624 | tf_op jit(solution)/shard_map/all_gather | solution.py:50
  110.8 7.0 %convolution_convert_fusion.2 = bf16[256,512]{1,0:T(8,128)(2,1)S(1)} fusion(bf16[256,8192]{1,0:T(8,128)(2,1)} %param.10, bf16[8192,512]{1,0:T(8,128)(2,1)} %all-gather.7.cloned.1.call-done), kind=kOutput, calls=%fused_computation.21 | convolution fusion | flops 2147614720 | bytes 12845056 | tf_op jit(solution)/shard_map/dot_general | solution.py:51
  117.9 1.1 fusion.19
  119.0 73.8 %all-gather.9.cloned.1.call-done = bf16[256,64,128]{2,1,0:T(8,128)(2,1)} async-done(((bf16[8,64,128]{2,1,0:T(8,128)(2,1)}), bf16[256,64,128]{2,1,0:T(8,128)(2,1)}) %all-gather.9.cloned.1.call-update) | async-done | bytes 4194320 | tf_op jit(solution)/shard_map/all_gather | solution.py:13
  192.8 34.2 %while.40 = (s32[]{:T(128)}, f32[8,64,128]{2,1,0:T(8,128)S(1)}, s32[]{:T(128)}, bf16[32,8]{1,0:T(8,128)(2,1)S(1)}, bf16[32,8,64,128]{3,2,1,0:T(8,128)(2,1)}, /*index=5*/s32[]{:T(128)}, s32[]{:T(128)}, s32[]{:T(128)}, s32[]{:T(128)}) while((s32[]{:T(128)}, f32[8,64,128]{2,1,0:T(8,128)S(1)}, s32[]{:T(128)}, ...), condition=%wide.region_1.2_spmd.clone, body=%wide.region_0.1_spmd.clone.sunk | while | flops 327696 | bytes 655607 | solution.py:31
  206.7 1.0 fusion.66
  227.5 1.6 fusion.15
  229.1 1.0 convolution_bitcast_fusion.2
  231.8 43.3 %all-gather.11.cloned.1.call-done = bf16[256,64,128]{2,1,0:T(8,128)(2,1)} async-done(((bf16[8,64,128]{2,1,0:T(8,128)(2,1)}), bf16[256,64,128]{2,1,0:T(8,128)(2,1)}) %all-gather.11.cloned.1.call-update) | async-done | bytes 4194320 | tf_op jit(solution)/shard_map/all_gather | solution.py:13
  275.1 33.7 %while.41 = (s32[]{:T(128)}, f32[8,64,128]{2,1,0:T(8,128)S(1)}, s32[]{:T(128)}, bf16[32,8]{1,0:T(8,128)(2,1)S(1)}, bf16[32,8,64,128]{3,2,1,0:T(8,128)(2,1)}, /*index=5*/s32[]{:T(128)}, s32[]{:T(128)}) while((s32[]{:T(128)}, f32[8,64,128]{2,1,0:T(8,128)S(1)}, s32[]{:T(128)}, bf16[32,8]{1,0:T(8,128)(2,1)S(1)}, ...), condition=%wide.region_7.8_spmd.clone, body=%wide.region_6.7_spmd.clone.sunk | while | flops 327692 | bytes 655545 | solution.py:31
  308.8 1.0 convolution_bitcast_fusion.1
  309.8 1.0 fusion.21
  310.9 7.8 %fusion.2 = bf16[8192,512]{0,1:T(8,128)(2,1)} fusion(bf16[256,512]{0,1:T(8,128)(2,1)S(1)} %bitcast.107, bf16[256,8192]{1,0:T(8,128)(2,1)} %param.10), kind=kOutput, calls=%fused_computation.7 | convolution fusion | flops 2151677952 | bytes 12845056 | tf_op jit(solution)/shard_map/dot_general | solution.py:106
  319.0 7.8 %convolution_convert_fusion.1 = bf16[256,8192]{1,0:T(8,128)(2,1)} fusion(bf16[256,512]{0,1:T(8,128)(2,1)S(1)} %bitcast.108, bf16[8192,512]{1,0:T(8,128)(2,1)} %all-gather.7.cloned.1.call-done), kind=kOutput, calls=%fused_computation.8 | convolution fusion | flops 2149580800 | bytes 12845056 | tf_op jit(solution)/shard_map/dot_general | solution.py:99
  326.8 47.2 %all-reduce.3.cloned.1.call-done = (bf16[256,128]{1,0:T(8,128)(2,1)}, bf16[256,128]{1,0:T(8,128)(2,1)}) async-done(((bf16[256,128]{1,0:T(8,128)(2,1)}, bf16[256,128]{1,0:T(8,128)(2,1)}), (bf16[256,128]{1,0:T(8,128)(2,1)}, bf16[256,128]{1,0:T(8,128)(2,1)})) %all-reduce.3.cloned.1.call-update) | async-done | bytes 131088 | tf_op jit(solution)/shard_map/psum | solution.py:96
  373.9 1.5 convert_element_type.131
  375.5 1.5 convert_element_type.135
  377.0 229.8 %reduce-scatter.5.cloned.1.call-done = bf16[256,512]{0,1:T(8,128)(2,1)} async-done(((bf16[8192,512]{0,1:T(8,128)(2,1)}), bf16[256,512]{0,1:T(8,128)(2,1)}) %reduce-scatter.5.cloned.1.call-update) | async-done | bytes 262160 | tf_op jit(solution)/shard_map/reduce_scatter | solution.py:105
  606.7 1.9 copy.31
  608.6 40.7 %reduce-scatter.3.cloned.1.call-done = bf16[256,1024]{1,0:T(8,128)(2,1)} async-done(((bf16[256,8192]{1,0:T(8,128)(2,1)}), bf16[256,1024]{1,0:T(8,128)(2,1)}) %reduce-scatter.3.cloned.1.call-update) | async-done | bytes 524304 | tf_op jit(solution)/shard_map/reduce_scatter | solution.py:102
  (157 shorter events, 69.4 us)
Async XLA Ops:
  7.2 46.8 %copy-start = (bf16[256,128]{1,0:T(8,128)(2,1)S(1)}, bf16[256,128]{1,0:T(8,128)(2,1)}, u32[]{:S(2)}) copy-start(bf16[256,128]{1,0:T(8,128)(2,1)} %param.13) | copy-start | bytes 196612
  7.2 103.6 %all-gather.7.cloned.1.call-start = ((), (), s32[]{:S(2)}) async-start(), calls=%async_computation.2 | async-start | bytes 8650752 | tf_op jit(solution)/shard_map/all_gather | solution.py:50
  7.9 184.9 %all-gather.9.cloned.1.call-start = ((), (), s32[]{:S(2)}) async-start(), calls=%async_computation.5 | async-start | bytes 4325376 | tf_op jit(solution)/shard_map/all_gather | solution.py:13
  12.2 262.9 %all-gather.11.cloned.1.call-start = ((), (), s32[]{:S(2)}) async-start(), calls=%async_computation.6 | async-start | bytes 4325376 | tf_op jit(solution)/shard_map/all_gather | solution.py:13
  119.0 255.0 %all-reduce.3.cloned.1.call-start = ((), (), s32[]{:S(2)}) async-start(), calls=%async_computation.7 | async-start | bytes 262144 | tf_op jit(solution)/shard_map/psum | solution.py:96
  227.0 3.8 copy-start.1
  310.9 295.9 %reduce-scatter.5.cloned.1.call-start = ((), (), s32[]{:S(2)}) async-start(), calls=%async_computation.4 | async-start | bytes 8650752 | tf_op jit(solution)/shard_map/reduce_scatter | solution.py:105
  318.7 330.6 %reduce-scatter.3.cloned.1.call-start = ((), (), s32[]{:S(2)}) async-start(), calls=%async_computation.3 | async-start | bytes 4718592 | tf_op jit(solution)/shard_map/reduce_scatter | solution.py:102
Sparse Core Ops, SparseCore 0:
  10.6 100.1 all-gather.6
  113.9 78.8 all-gather.8
  196.0 79.0 all-gather.10
  311.0 62.9 all-reduce.2
  378.4 228.3 reduce-scatter.4
  609.7 39.6 reduce-scatter.2
where the time goes:
time: 658 us; the launch traced here: 656 us
  waiting for transfers between devices  491 us (75%)
  other arithmetic  68.8 us (10%)
  blocking collectives  41.5 us (6%)
  matrix products  34.2 us (5%)
  between operations  14.3 us (2%)
    reduce_scatter x1, waiting for transfers between devices, per_device(): lax.psum_scatter(lax.dot_general(inputs, grad_values, (((0,), (0,)), ((),...  230 us
    all_gather x2, waiting for transfers between devices, carried_in(): lax.all_gather(part.astype(kind), axis)  117 us
    select_n x64, other arithmetic, lap(): return jax.tree.map(lambda a, b: jnp.where(reached, a, b), new, before)  64.9 us
    all_gather x1, waiting for transfers between devices, per_device(): w_full = lax.all_gather(w_value, 'seq', axis=0, tiled=True)  55.8 us
    psum x1, waiting for transfers between devices, per_device(): lax.psum(grad_b.reshape(steps, states).astype(jnp.bfloat16), 'head')  47.2 us
    all_gather x1, blocking collectives, carried_in(): lax.all_gather(part.astype(kind), axis)  41.5 us
    reduce_scatter x1, waiting for transfers between devices, per_device(): lax.psum_scatter(term.astype(jnp.bfloat16), 'head', scatter_dimension=1,...  40.7 us
  transfers between devices with their start and end apart: 6, of which 6 were waited for; matrix products, arithmetic and copies ran while one was open for 11% of the time, Pallas kernels for 0%

commit v1 on v0

--- a/solution.py
+++ b/solution.py
@@ -47,7 +47,9 @@
     depth = columns // heads
     states = b_proj.shape[1]
     blocks = steps // SPAN
-    w_full = lax.all_gather(w_value, "seq", axis=0, tiled=True)
+    w_full = jnp.concatenate(
+        lax.all_to_all(jnp.stack([w_value] * lax.axis_size("seq")), "seq", 0, 0), axis=0
+    )
     values = jnp.dot(inputs, w_full, preferred_element_type=jnp.float32).astype(jnp.bfloat16)
     xs = values.astype(jnp.float32).reshape(blocks, SPAN, heads, depth)
     dys = grad_out.astype(jnp.float32).reshape(blocks, SPAN, heads, depth)

time: 658 us -> 734 us (1.12)
  blocking collectives: 41.5 us -> 238 us
  waiting for transfers between devices: 491 us -> 358 us
  starting transfers between devices: 0.42 us -> 12.3 us
    all_gather x1, blocking collectives: 41.5 us -> 238 us  [carried_in(): lax.all_gather(part.astype(kind), axis)]
    all_gather x2, waiting for transfers between devices: 117 us -> 39.8 us  [carried_in(): lax.all_gather(part.astype(kind), axis)]
    all_gather x1 -> x0, waiting for transfers between devices: 55.8 us -> none  [per_device(): w_full = lax.all_gather(w_value, 'seq', axis=0, tiled=True)]
    all_to_all x0 -> x1, starting transfers between devices: none -> 11.9 us  [per_device(): lax.all_to_all(jnp.stack([w_value] * lax.axis_size('seq')), 'seq', 0, 0)]
  transfers between devices with their start and end apart: 6 -> 6, of which waited for: 6 -> 4; matrix products, arithmetic and copies ran while one was open for 11% -> 9% of each run, Pallas kernels for 0% -> 0%
where the time goes in v1:
time: 734 us; the launch traced here: 733 us
  waiting for transfers between devices  358 us (49%)
  blocking collectives  238 us (32%)
  other arithmetic  68.8 us (9%)
  matrix products  31.8 us (4%)
  between operations  14 us (2%)
  starting transfers between devices  12.3 us (2%)
  local copies, waits for them, and re-layouts  7.65 us (1%)
    all_gather x1, blocking collectives, carried_in(): lax.all_gather(part.astype(kind), axis)  238 us
    reduce_scatter x1, waiting for transfers between devices, per_device(): lax.psum_scatter(lax.dot_general(inputs, grad_values, (((0,), (0,)), ((),...  230 us
    select_n x64, other arithmetic, lap(): return jax.tree.map(lambda a, b: jnp.where(reached, a, b), new, before)  65 us
    psum x1, waiting for transfers between devices, per_device(): lax.psum(grad_b.reshape(steps, states).astype(jnp.bfloat16), 'head')  47.2 us
    reduce_scatter x1, waiting for transfers between devices, per_device(): lax.psum_scatter(term.astype(jnp.bfloat16), 'head', scatter_dimension=1,...  40.8 us
    all_gather x2, waiting for transfers between devices, carried_in(): lax.all_gather(part.astype(kind), axis)  39.8 us
  transfers between devices with their start and end apart: 6, of which 4 were waited for; matrix products, arithmetic and copies ran while one was open for 9% of the time, Pallas kernels for 0%

profile of v1, /device:TPU:8, one launch (start us, length us, event | category | flops | bytes accessed | tf_op | source)
XLA Modules:
  0.0 732.6 jit_solution(6471090843430099672)
XLA Ops:
  7.2 5.2 stack.2
  12.3 11.9 %all-to-all-start = ((bf16[32,256,512]{2,1,0:T(8,128)(2,1)}), bf16[32,256,512]{2,1,0:T(8,128)(2,1)}, u32[]{:S(2)}, u32[]{:S(2)}) async-start(bf16[32,256,512]{2,1,0:T(8,128)(2,1)} %stack.2), calls=%async_computation | async-start | bytes 16777216 | tf_op jit(solution)/shard_map/all_to_all | solution.py:51
  24.9 1.1 fusion.18
  26.3 238.1 %all-gather = bf16[32,1,8]{2,1,0:T(2,128)(2,1)S(1)} all-gather(bf16[1,1,8]{2,1,0:T(2,128)(2,1)S(1)} %copy.26), channel_id=2, replica_groups=mesh['seq'=32,'head'=8] {'seq'}, dimensions={0}, use_global_device_ids=true | all-gather | bytes 528 | tf_op jit(solution)/shard_map/all_gather | solution.py:13
  264.7 7.0 convolution_convert_fusion.2
  271.8 1.1 fusion.19
  273.0 34.3 %while.40 = (s32[]{:T(128)}, f32[8,64,128]{2,1,0:T(8,128)S(1)}, s32[]{:T(128)}, bf16[32,8]{1,0:T(8,128)(2,1)S(1)}, bf16[32,8,64,128]{3,2,1,0:T(8,128)(2,1)}, /*index=5*/s32[]{:T(128)}, s32[]{:T(128)}, s32[]{:T(128)}, s32[]{:T(128)}) while((s32[]{:T(128)}, f32[8,64,128]{2,1,0:T(8,128)S(1)}, s32[]{:T(128)}, ...), condition=%wide.region_1.2_spmd.clone, body=%wide.region_0.1_spmd.clone.sunk | while | flops 327696 | bytes 655607 | solution.py:31
  282.7 1.0 fusion.66
  289.1 1.0 fusion.66
  296.6 1.0 fusion.66
  307.7 1.6 fusion.15
  309.3 1.0 convolution_bitcast_fusion.2
  312.0 39.8 %all-gather.8.cloned.1.call-done = bf16[256,64,128]{2,1,0:T(8,128)(2,1)} async-done(((bf16[8,64,128]{2,1,0:T(8,128)(2,1)}), bf16[256,64,128]{2,1,0:T(8,128)(2,1)}) %all-gather.8.cloned.1.call-update) | async-done | bytes 4194320 | tf_op jit(solution)/shard_map/all_gather | solution.py:13
  351.7 33.7 %while.41 = (s32[]{:T(128)}, f32[8,64,128]{2,1,0:T(8,128)S(1)}, s32[]{:T(128)}, bf16[32,8]{1,0:T(8,128)(2,1)S(1)}, bf16[32,8,64,128]{3,2,1,0:T(8,128)(2,1)}, /*index=5*/s32[]{:T(128)}, s32[]{:T(128)}) while((s32[]{:T(128)}, f32[8,64,128]{2,1,0:T(8,128)S(1)}, s32[]{:T(128)}, bf16[32,8]{1,0:T(8,128)(2,1)S(1)}, ...), condition=%wide.region_7.8_spmd.clone, body=%wide.region_6.7_spmd.clone.sunk | while | flops 327692 | bytes 655545 | solution.py:31
  385.4 1.0 convolution_bitcast_fusion.1
  386.5 1.0 fusion.21
  387.7 7.8 %fusion.2 = bf16[8192,512]{0,1:T(8,128)(2,1)} fusion(bf16[256,512]{0,1:T(8,128)(2,1)S(1)} %bitcast.108, bf16[256,8192]{1,0:T(8,128)(2,1)} %param.10), kind=kOutput, calls=%fused_computation.7 | convolution fusion | flops 2151677952 | bytes 12845056 | tf_op jit(solution)/shard_map/dot_general | solution.py:108
  395.6 7.8 %convolution_convert_fusion.1 = bf16[256,8192]{1,0:T(8,128)(2,1)} fusion(bf16[256,512]{0,1:T(8,128)(2,1)S(1)} %bitcast.109, bf16[8192,512]{1,0:T(8,128)(2,1)} %bitcast.19), kind=kOutput, calls=%fused_computation.8 | convolution fusion | flops 2149580800 | bytes 12845056 | tf_op jit(solution)/shard_map/dot_general | solution.py:101
  403.4 47.2 %all-reduce.3.cloned.1.call-done = (bf16[256,128]{1,0:T(8,128)(2,1)}, bf16[256,128]{1,0:T(8,128)(2,1)}) async-done(((bf16[256,128]{1,0:T(8,128)(2,1)}, bf16[256,128]{1,0:T(8,128)(2,1)}), (bf16[256,128]{1,0:T(8,128)(2,1)}, bf16[256,128]{1,0:T(8,128)(2,1)})) %all-reduce.3.cloned.1.call-update) | async-done | bytes 131088 | tf_op jit(solution)/shard_map/psum | solution.py:98
  450.6 1.5 convert_element_type.132
  452.1 1.5 convert_element_type.136
  453.6 229.8 %reduce-scatter.5.cloned.1.call-done = bf16[256,512]{0,1:T(8,128)(2,1)} async-done(((bf16[8192,512]{0,1:T(8,128)(2,1)}), bf16[256,512]{0,1:T(8,128)(2,1)}) %reduce-scatter.5.cloned.1.call-update) | async-done | bytes 262160 | tf_op jit(solution)/shard_map/reduce_scatter | solution.py:107
  683.4 1.9 copy.31
  685.2 40.8 %reduce-scatter.3.cloned.1.call-done = bf16[256,1024]{1,0:T(8,128)(2,1)} async-done(((bf16[256,8192]{1,0:T(8,128)(2,1)}), bf16[256,1024]{1,0:T(8,128)(2,1)}) %reduce-scatter.3.cloned.1.call-update) | async-done | bytes 524304 | tf_op jit(solution)/shard_map/reduce_scatter | solution.py:104
  (161 shorter events, 66.3 us)
Async XLA Ops:
  7.2 257.3 %copy-start = (bf16[256,128]{1,0:T(8,128)(2,1)S(1)}, bf16[256,128]{1,0:T(8,128)(2,1)}, u32[]{:S(2)}) copy-start(bf16[256,128]{1,0:T(8,128)(2,1)} %param.13) | copy-start | bytes 196612
  12.3 12.0 %copy-start.2 = (bf16[256,512]{1,0:T(8,128)(2,1)S(1)}, bf16[256,512]{1,0:T(8,128)(2,1)}, u32[]{:S(2)}) copy-start(bf16[256,512]{1,0:T(8,128)(2,1)} %param.15) | copy-start | bytes 786436
  12.3 12.1 %copy-start.3 = (f32[256,8]{0,1:T(8,128)S(1)}, f32[256,8]{0,1:T(8,128)}, u32[]{:S(2)}) copy-start(f32[256,8]{0,1:T(8,128)} %param.12) | copy-start | bytes 24580
  12.3 12.6 %copy-start.1 = (bf16[256,128]{1,0:T(8,128)(2,1)S(1)}, bf16[256,128]{1,0:T(8,128)(2,1)}, u32[]{:S(2)}) copy-start(bf16[256,128]{1,0:T(8,128)(2,1)} %param.14) | copy-start | bytes 196612
  12.3 252.3 %all-to-all-start = ((bf16[32,256,512]{2,1,0:T(8,128)(2,1)}), bf16[32,256,512]{2,1,0:T(8,128)(2,1)}, u32[]{:S(2)}, u32[]{:S(2)}) async-start(bf16[32,256,512]{2,1,0:T(8,128)(2,1)} %stack.2), calls=%async_computation | async-start | bytes 16777216 | tf_op jit(solution)/shard_map/all_to_all | solution.py:51
  24.2 248.7 %all-gather.6.cloned.1.call-start = ((), (), s32[]{:S(2)}) async-start(), calls=%async_computation.5 | async-start | bytes 4325376 | tf_op jit(solution)/shard_map/all_gather | solution.py:13
  26.0 325.7 %all-gather.8.cloned.1.call-start = ((), (), s32[]{:S(2)}) async-start(), calls=%async_computation.6 | async-start | bytes 4325376 | tf_op jit(solution)/shard_map/all_gather | solution.py:13
  272.9 177.7 %all-reduce.3.cloned.1.call-start = ((), (), s32[]{:S(2)}) async-start(), calls=%async_computation.7 | async-start | bytes 262144 | tf_op jit(solution)/shard_map/psum | solution.py:98
  387.5 295.8 %reduce-scatter.5.cloned.1.call-start = ((), (), s32[]{:S(2)}) async-start(), calls=%async_computation.4 | async-start | bytes 8650752 | tf_op jit(solution)/shard_map/reduce_scatter | solution.py:107
  395.6 330.5 %reduce-scatter.3.cloned.1.call-start = ((), (), s32[]{:S(2)}) async-start(), calls=%async_computation.3 | async-start | bytes 4718592 | tf_op jit(solution)/shard_map/reduce_scatter | solution.py:104
Sparse Core Ops, SparseCore 0:
  28.2 141.5 all-gather.5
  273.0 78.6 all-gather.7
  387.6 62.9 all-reduce.2
  455.0 228.3 reduce-scatter.4
  686.3 39.6 reduce-scatter.2
